TPU v7x, 512 devices: a whole 4x8x8 slice. The times are simulated.
512 devices in a mesh: leaf: 16 (over y, core), blk: 32 (over z, x).
Axes of the slice: x: 4, y: 8, z: 8, core: 2. Of those that a mesh axis runs over, the one named last changes fastest.
Arguments:
- adjoint_rhs: float32 [128, 128, 64], P('leaf'), may hold values from -6 to 6
- diag_inverse: float32 [128, 128, 128], P('leaf'), may hold values from -1 to 2
- blocks: float32 [16, 32, 32, 128, 128], P('leaf', 'blk'), may hold values from -0.03125 to 0.03125
- block_rows: int32 [16, 32, 32], P('leaf', 'blk'), may hold values from 0 to 127, as said below
- block_cols: int32 [16, 32, 32], P('leaf', 'blk'), may hold values from 0 to 7
- block_count: int32 [16, 32], P('leaf', 'blk'), may hold values from 0 to 32, as said below
- node_level: int32 [16], replicated, may hold values from 0 to 3, as said below
Outputs:
- adjoint_solution: float32 [128, 128, 64], P('leaf')
Inputs may be any that keep to these rules, and one draw needn't show every extreme that they name: `node_level`: exactly one node has level 0, and every level up to 3 is held by some node. `block_rows`: every live slot names a block row of a node whose level is lower than that of the slot's own node. `block_count`: the node of level 0 has no live slots; every other node has one device with exactly 32 live slots.
All inputs are finite; a program needn't handle non-finite values.
Results may differ from a plain program's by a relative error of at most 0.0003.
Values sent between devices are 32-bit elements; how exact they have to be, the bound alone decides.
A program may use at most 64 MiB of HBM per device.

v0:
```python
import jax
import jax.numpy as jnp
from jax import lax
from jax.sharding import PartitionSpec as P

LEVELS = 4


def accumulate(solved_all, tiles, row_ids, col_ids, trip_count, partial_shape):

    def add_tile(slot_at, partial_value):
        tile = lax.dynamic_index_in_dim(tiles, slot_at, 0, keepdims=False)
        row_at = lax.dynamic_index_in_dim(row_ids, slot_at, 0, keepdims=False)
        col_at = lax.dynamic_index_in_dim(col_ids, slot_at, 0, keepdims=False)
        panel_row = lax.dynamic_index_in_dim(solved_all, row_at, 0, keepdims=False)
        product = lax.dot_general(
            tile, panel_row, (((0,), (0,)), ((), ())), precision=lax.Precision.HIGHEST
        )
        current = lax.dynamic_index_in_dim(partial_value, col_at, 0, keepdims=False)
        return lax.dynamic_update_index_in_dim(partial_value, current + product, col_at, 0)

    return lax.fori_loop(0, trip_count, add_tile, jnp.zeros(partial_shape, jnp.float32))


def body(adjoint_rhs, diag_inverse, blocks, block_rows, block_cols, block_count, node_level):
    per_node, width, columns = adjoint_rhs.shape
    capacity = blocks.shape[2]
    leaves = lax.axis_size("leaf")
    my_depth = lax.dynamic_index_in_dim(node_level, lax.axis_index("leaf"), 0, keepdims=False)
    tiles = blocks.reshape(capacity, width, width)
    row_ids = block_rows.reshape(capacity)
    col_ids = block_cols.reshape(capacity)
    live_count = block_count.reshape(())
    solved_all = jnp.zeros((leaves * per_node, width, columns), jnp.float32)
    own_solution = jnp.zeros_like(adjoint_rhs)
    for section_level in range(LEVELS):
        active = my_depth == section_level
        trip_count = jnp.where(active, live_count, 0)
        partial_value = accumulate(
            solved_all, tiles, row_ids, col_ids, trip_count, (per_node, width, columns)
        )
        summed = lax.psum(partial_value, "blk")
        updated = jnp.einsum(
            "cij,cjk->cik", diag_inverse, adjoint_rhs - summed, precision=lax.Precision.HIGHEST
        )
        own_solution = jnp.where(active, updated, own_solution)
        if section_level + 1 < LEVELS:
            solved_all = lax.all_gather(own_solution, "leaf", axis=0, tiled=True)
    return own_solution


def solution(mesh):
    in_specs = (
        P("leaf", None, None),
        P("leaf", None, None),
        P("leaf", "blk", None, None, None),
        P("leaf", "blk", None),
        P("leaf", "blk", None),
        P("leaf", "blk"),
        P(),
    )
    out_specs = P("leaf", None, None)
    return jax.shard_map(body, mesh=mesh, in_specs=in_specs, out_specs=out_specs, check_vma=False)
```

profile of v0, /device:TPU:8, one launch (start us, length us, event | category | flops | bytes accessed | tf_op | source)
XLA Modules:
  0.0 1508.8 jit_solution(4455952233501976158)
XLA Ops:
  7.3 1.3 dynamic_slice.67
  9.3 0.7 copy-done.3
  10.0 0.0 all-gather.4.cloned.1.call-start
  10.0 160.8 %all-reduce.5.cloned.1.call-done = f32[8,128,64]{1,2,0:T(8,128)} async-done(((f32[8,128,64]{1,2,0:T(8,128)}), f32[8,128,64]{1,2,0:T(8,128)}) %all-reduce.5.cloned.1.call-update) | async-done | bytes 262160 | tf_op jit(solution)/shard_map/psum | solution.py:42
  170.8 2.8 fusion.31
  174.4 40.5 %all-gather.4.cloned.1.call-done = f32[128,128,64]{1,2,0:T(8,128)} async-done(((f32[8,128,64]{1,2,0:T(8,128)}), f32[128,128,64]{1,2,0:T(8,128)}) %all-gather.4.cloned.1.call-update) | async-done | bytes 4194320 | tf_op jit(solution)/shard_map/all_gather | solution.py:48
  214.9 77.4 %while.42 = (s32[]{:T(128)}, f32[8,128,64]{1,2,0:T(8,128)S(1)}, s32[]{:T(128)}, s32[32]{0:T(128)}, f32[32,128,128]{2,1,0:T(8,128)}, /*index=5*/s32[32]{0:T(128)}...) while((s32[]{:T(128)}, f32[8,128,64]{1,2,0:T(8,128)S(1)}, ...), condition=%wide.region_4.5_spmd, body=%wide.region_3.4_spmd.sunk | while | flops 12591115 | bytes 229635 | solution.py:22
  214.9 1.3 dynamic_slice.124
  218.3 1.3 dynamic_slice.125
  221.6 1.0 fusion.57
  222.7 1.3 dynamic_slice.124
  226.0 1.3 dynamic_slice.125
  229.3 1.0 fusion.57
  230.4 1.3 dynamic_slice.124
  233.8 1.3 dynamic_slice.125
  237.1 1.0 fusion.57
  238.1 1.3 dynamic_slice.124
  241.5 1.3 dynamic_slice.125
  244.8 1.0 fusion.57
  245.9 1.3 dynamic_slice.124
  249.2 1.3 dynamic_slice.125
  252.6 1.0 fusion.57
  253.6 1.3 dynamic_slice.124
  257.0 1.3 dynamic_slice.125
  260.3 1.0 fusion.57
  261.4 1.3 dynamic_slice.124
  264.7 1.3 dynamic_slice.125
  268.0 1.0 fusion.57
  269.1 1.3 dynamic_slice.124
  272.5 1.3 dynamic_slice.125
  275.8 1.0 fusion.57
  276.9 1.3 dynamic_slice.124
  280.2 1.3 dynamic_slice.125
  283.5 1.0 fusion.57
  284.6 1.3 dynamic_slice.124
  287.9 1.3 dynamic_slice.125
  291.3 1.0 fusion.57
  292.3 0.7 copy-done.4
  293.1 324.3 %all-reduce.7.cloned.1.call-done = f32[8,128,64]{1,2,0:T(8,128)} async-done(((f32[8,128,64]{1,2,0:T(8,128)}), f32[8,128,64]{1,2,0:T(8,128)}) %all-reduce.7.cloned.1.call-update) | async-done | bytes 262160 | tf_op jit(solution)/shard_map/psum | solution.py:42
  617.4 2.8 fusion.30
  620.9 40.5 %all-gather.6.cloned.1.call-done = f32[128,128,64]{1,2,0:T(8,128)} async-done(((f32[8,128,64]{1,2,0:T(8,128)}), f32[128,128,64]{1,2,0:T(8,128)}) %all-gather.6.cloned.1.call-update) | async-done | bytes 4194320 | tf_op jit(solution)/shard_map/all_gather | solution.py:48
  661.5 0.7 copy-done.5
  662.2 401.4 %all-reduce.9.cloned.1.call-done = f32[8,128,64]{1,2,0:T(8,128)} async-done(((f32[8,128,64]{1,2,0:T(8,128)}), f32[8,128,64]{1,2,0:T(8,128)}) %all-reduce.9.cloned.1.call-update) | async-done | bytes 262160 | tf_op jit(solution)/shard_map/psum | solution.py:42
  1063.6 2.9 fusion.29
  1067.2 40.4 %all-gather.8.cloned.1.call-done = f32[128,128,64]{1,2,0:T(8,128)} async-done(((f32[8,128,64]{1,2,0:T(8,128)}), f32[128,128,64]{1,2,0:T(8,128)}) %all-gather.8.cloned.1.call-update) | async-done | bytes 4194320 | tf_op jit(solution)/shard_map/all_gather | solution.py:48
  1107.6 0.7 copy-done.2
  1108.3 390.8 %all-reduce.11.cloned.1.call-done = f32[8,128,64]{1,2,0:T(8,128)} async-done(((f32[8,128,64]{1,2,0:T(8,128)}), f32[8,128,64]{1,2,0:T(8,128)}) %all-reduce.11.cloned.1.call-update) | async-done | bytes 262160 | tf_op jit(solution)/shard_map/psum | solution.py:42
  1499.1 2.9 fusion.28
  (38 shorter events, 0.5 us)
Async XLA Ops:
  6.5 164.3 %copy-start = (f32[8,128,128]{2,1,0:T(8,128)S(1)}, f32[8,128,128]{2,1,0:T(8,128)}, u32[]{:S(2)}) copy-start(f32[8,128,128]{2,1,0:T(8,128)} %param.16) | copy-start | bytes 1572868
  6.5 610.8 %copy-start.1 = (f32[8,128,64]{1,2,0:T(8,128)S(1)}, f32[8,128,64]{1,2,0:T(8,128)}, u32[]{:S(2)}) copy-start(f32[8,128,64]{1,2,0:T(8,128)} %param.15) | copy-start | bytes 786436
  6.5 164.3 %all-reduce.5.cloned.1.call-start = ((), (), s32[]{:S(2)}) async-start(), calls=%async_computation | async-start | bytes 524288 | tf_op jit(solution)/shard_map/psum | solution.py:42
  9.3 0.7 copy-start.3
  10.0 204.9 %all-gather.4.cloned.1.call-start = ((), (), s32[]{:S(2)}) async-start(), calls=%async_computation.1 | async-start | bytes 4456448 | tf_op jit(solution)/shard_map/all_gather | solution.py:48
  173.7 443.6 %all-reduce.7.cloned.1.call-start = ((), (), s32[]{:S(2)}) async-start(), calls=%async_computation.2 | async-start | bytes 524288 | tf_op jit(solution)/shard_map/psum | solution.py:42
  292.3 0.7 copy-start.4
  293.0 368.4 %all-gather.6.cloned.1.call-start = ((), (), s32[]{:S(2)}) async-start(), calls=%async_computation.3 | async-start | bytes 4456448 | tf_op jit(solution)/shard_map/all_gather | solution.py:48
  620.2 443.4 %all-reduce.9.cloned.1.call-start = ((), (), s32[]{:S(2)}) async-start(), calls=%async_computation.4 | async-start | bytes 524288 | tf_op jit(solution)/shard_map/psum | solution.py:42
  661.4 0.7 copy-start.5
  662.2 445.4 %all-gather.8.cloned.1.call-start = ((), (), s32[]{:S(2)}) async-start(), calls=%async_computation.5 | async-start | bytes 4456448 | tf_op jit(solution)/shard_map/all_gather | solution.py:48
  1066.5 432.6 %all-reduce.11.cloned.1.call-start = ((), (), s32[]{:S(2)}) async-start(), calls=%async_computation.6 | async-start | bytes 524288 | tf_op jit(solution)/shard_map/psum | solution.py:42
  1107.6 0.7 copy-start.2
Sparse Core Ops, SparseCore 0:
  10.8 159.9 all-reduce.4
  173.8 40.9 all-gather.3
  293.2 324.1 all-reduce.6
  620.3 41.0 all-gather.5
  664.7 398.8 all-reduce.8
  1066.6 40.9 all-gather.7
  1111.0 388.0 all-reduce.10
where the time goes:
time: 1510 us
  waiting for transfers between devices  1400 us (93%)
  loops' own time  40.9 us (3%)
  local copies, waits for them, and re-layouts  30.4 us (2%)
  matrix products  21.6 us (1%)
  between operations  16.9 us (1%)
    psum x4, waiting for transfers between devices, body(): summed = lax.psum(partial_value, 'blk')  1280 us
    all_gather x3, waiting for transfers between devices, body(): solved_all = lax.all_gather(own_solution, 'leaf', axis=0, tiled=True)  121 us
    another operation x4, loops' own time, accumulate(): lax.fori_loop(0, trip_count, add_tile, jnp.zeros(partial_shape, jnp.float...  40.9 us
  transfers between devices with their start and end apart: 7, of which 7 were waited for; matrix products, arithmetic and copies ran while one was open for 0% of the time, Pallas kernels for 0%

commit v1 on v0

--- a/solution.py
+++ b/solution.py
@@ -39,7 +39,7 @@
         partial_value = accumulate(
             solved_all, tiles, row_ids, col_ids, trip_count, (per_node, width, columns)
         )
-        summed = lax.psum(partial_value, "blk")
+        summed = jnp.sum(lax.all_gather(partial_value, "blk"), axis=0)
         updated = jnp.einsum(
             "cij,cjk->cik", diag_inverse, adjoint_rhs - summed, precision=lax.Precision.HIGHEST
         )

time: 1510 us -> 1170 us (0.77)
  the two profiles are of different devices: /device:TPU:8 before, /device:TPU:1 now
where the time goes in v1:
time: 1170 us
  waiting for transfers between devices  939 us (80%)
  loops' own time  117 us (10%)
  local copies, waits for them, and re-layouts  41.5 us (4%)
  matrix products  39.3 us (3%)
  between operations  16.6 us (1%)
  other arithmetic  16.1 us (1%)
    all_gather x4, waiting for transfers between devices, body(): summed = jnp.sum(lax.all_gather(partial_value, 'blk'), axis=0)  814 us
    all_gather x3, waiting for transfers between devices, body(): solved_all = lax.all_gather(own_solution, 'leaf', axis=0, tiled=True)  125 us
    another operation x4, loops' own time, accumulate(): lax.fori_loop(0, trip_count, add_tile, jnp.zeros(partial_shape, jnp.float...  117 us
    dot_general x31, matrix products, add_tile(): lax.dot_general(tile, panel_row, (((0,), (0,)), ((), ())), precision=lax....  32 us
  transfers between devices with their start and end apart: 7, of which 7 were waited for; matrix products, arithmetic and copies ran while one was open for 0% of the time, Pallas kernels for 0%

profile of v1, /device:TPU:1, one launch (start us, length us, event | category | flops | bytes accessed | tf_op | source)
XLA Modules:
  0.0 1169.9 jit_solution(13038945921283084803)
XLA Ops:
  7.2 1.2 dynamic_slice.67
  9.8 110.4 %all-gather.18.cloned.1.call-done = f32[256,128,64]{1,2,0:T(8,128)} async-done(((f32[8,128,64]{1,2,0:T(8,128)}), f32[256,128,64]{1,2,0:T(8,128)}) %all-gather.18.cloned.1.call-update) | async-done | bytes 8388624 | tf_op jit(solution)/shard_map/all_gather | solution.py:42
  120.2 4.0 reduce_sum.36
  124.2 1.8 fusion.31
  126.7 41.5 %all-gather.12.cloned.1.call-done = f32[128,128,64]{1,2,0:T(8,128)} async-done(((f32[8,128,64]{1,2,0:T(8,128)}), f32[128,128,64]{1,2,0:T(8,128)}) %all-gather.12.cloned.1.call-update) | async-done | bytes 4194320 | tf_op jit(solution)/shard_map/all_gather | solution.py:48
  169.1 298.6 %all-gather.20.cloned.1.call-done = f32[256,128,64]{1,2,0:T(8,128)} async-done(((f32[8,128,64]{1,2,0:T(8,128)}), f32[256,128,64]{1,2,0:T(8,128)}) %all-gather.20.cloned.1.call-update) | async-done | bytes 8388624 | tf_op jit(solution)/shard_map/all_gather | solution.py:42
  467.6 4.0 reduce_sum.37
  471.7 1.8 fusion.30
  474.1 41.5 %all-gather.14.cloned.1.call-done = f32[128,128,64]{1,2,0:T(8,128)} async-done(((f32[8,128,64]{1,2,0:T(8,128)}), f32[128,128,64]{1,2,0:T(8,128)}) %all-gather.14.cloned.1.call-update) | async-done | bytes 4194320 | tf_op jit(solution)/shard_map/all_gather | solution.py:48
  516.5 298.1 %all-gather.22.cloned.1.call-done = f32[256,128,64]{1,2,0:T(8,128)} async-done(((f32[8,128,64]{1,2,0:T(8,128)}), f32[256,128,64]{1,2,0:T(8,128)}) %all-gather.22.cloned.1.call-update) | async-done | bytes 8388624 | tf_op jit(solution)/shard_map/all_gather | solution.py:42
  814.6 4.0 reduce_sum.38
  818.6 1.8 fusion.29
  821.1 41.5 %all-gather.16.cloned.1.call-done = f32[128,128,64]{1,2,0:T(8,128)} async-done(((f32[8,128,64]{1,2,0:T(8,128)}), f32[128,128,64]{1,2,0:T(8,128)}) %all-gather.16.cloned.1.call-update) | async-done | bytes 4194320 | tf_op jit(solution)/shard_map/all_gather | solution.py:48
  862.6 186.9 %while.44 = (s32[]{:T(128)}, f32[8,128,64]{1,2,0:T(8,128)S(1)}, s32[]{:T(128)}, s32[32]{0:T(128)S(1)}, f32[32,128,128]{2,1,0:T(8,128)}, /*index=5*/s32[32]{0:T(1...) while((s32[]{:T(128)}, f32[8,128,64]{1,2,0:T(8,128)S(1)}, ...), condition=%wide.region_10.11_spmd, body=%wide.region_9.10_spmd.sunk | while | flops 12591115 | bytes 229635 | solution.py:22
  867.6 1.0 fusion.63
  873.7 1.0 fusion.63
  879.7 1.0 fusion.63
  885.7 1.0 fusion.63
  891.7 1.0 fusion.63
  897.8 1.0 fusion.63
  903.8 1.0 fusion.63
  909.8 1.0 fusion.63
  915.8 1.0 fusion.63
  921.9 1.0 fusion.63
  927.9 1.0 fusion.63
  933.9 1.0 fusion.63
  940.0 1.0 fusion.63
  946.0 1.0 fusion.63
  952.0 1.0 fusion.63
  958.0 1.0 fusion.63
  964.1 1.0 fusion.63
  970.1 1.0 fusion.63
  976.1 1.0 fusion.63
  982.1 1.0 fusion.63
  988.2 1.0 fusion.63
  994.2 1.0 fusion.63
  1000.2 1.0 fusion.63
  1006.3 1.0 fusion.63
  1012.3 1.0 fusion.63
  1018.3 1.0 fusion.63
  1024.3 1.0 fusion.63
  1030.4 1.0 fusion.63
  1036.4 1.0 fusion.63
  1042.4 1.0 fusion.63
  1048.4 1.0 fusion.63
  1050.2 107.0 %all-gather.24.cloned.1.call-done = f32[256,128,64]{1,2,0:T(8,128)} async-done(((f32[8,128,64]{1,2,0:T(8,128)}), f32[256,128,64]{1,2,0:T(8,128)}) %all-gather.24.cloned.1.call-update) | async-done | bytes 8388624 | tf_op jit(solution)/shard_map/all_gather | solution.py:42
  1157.2 4.0 reduce_sum.39
  1161.3 1.8 fusion.28
  (136 shorter events, 40.7 us)
Async XLA Ops:
  6.5 117.7 %copy-start = (f32[8,128,128]{2,1,0:T(8,128)S(1)}, f32[8,128,128]{2,1,0:T(8,128)}, u32[]{:S(2)}) copy-start(f32[8,128,128]{2,1,0:T(8,128)} %param.16) | copy-start | bytes 1572868
  6.5 113.7 %all-gather.18.cloned.1.call-start = ((), (), s32[]{:S(2)}) async-start(), calls=%async_computation.3 | async-start | bytes 8650752 | tf_op jit(solution)/shard_map/all_gather | solution.py:42
  9.1 0.7 copy-start.5
  9.8 158.4 %all-gather.12.cloned.1.call-start = ((), (), s32[]{:S(2)}) async-start(), calls=%async_computation | async-start | bytes 4456448 | tf_op jit(solution)/shard_map/all_gather | solution.py:48
  120.2 4.0 copy-start.1
  120.2 48.0 %copy-start.9 = (s32[32]{0:T(128)S(1)}, s32[32]{0:T(128)}, u32[]{:S(2)}) copy-start(s32[32]{0:T(128)} %get-tuple-element.590) | copy-start | bytes 388
  120.2 48.0 %copy-start.10 = (s32[1,1,32]{2,1,0:T(1,128)S(1)}, s32[1,1,32]{2,1,0:T(1,128)}, u32[]{:S(2)}) copy-start(s32[1,1,32]{2,1,0:T(1,128)} %param.18) | copy-start | bytes 388
  126.1 341.6 %all-gather.20.cloned.1.call-start = ((), (), s32[]{:S(2)}) async-start(), calls=%async_computation.4 | async-start | bytes 8650752 | tf_op jit(solution)/shard_map/all_gather | solution.py:42
  168.3 0.7 copy-start.6
  169.0 346.6 %all-gather.14.cloned.1.call-start = ((), (), s32[]{:S(2)}) async-start(), calls=%async_computation.1 | async-start | bytes 4456448 | tf_op jit(solution)/shard_map/all_gather | solution.py:48
  467.6 4.0 copy-start.2
  473.5 341.1 %all-gather.22.cloned.1.call-start = ((), (), s32[]{:S(2)}) async-start(), calls=%async_computation.5 | async-start | bytes 8650752 | tf_op jit(solution)/shard_map/all_gather | solution.py:42
  515.7 0.7 copy-start.7
  516.4 346.2 %all-gather.16.cloned.1.call-start = ((), (), s32[]{:S(2)}) async-start(), calls=%async_computation.2 | async-start | bytes 4456448 | tf_op jit(solution)/shard_map/all_gather | solution.py:48
  814.6 4.0 copy-start.4
  820.5 336.7 %all-gather.24.cloned.1.call-start = ((), (), s32[]{:S(2)}) async-start(), calls=%async_computation.6 | async-start | bytes 8650752 | tf_op jit(solution)/shard_map/all_gather | solution.py:42
  1049.5 0.7 copy-start.8
  1157.2 4.0 copy-start.3
Sparse Core Ops, SparseCore 0:
  10.5 109.6 all-gather.17
  126.2 41.9 all-gather.11
  171.4 296.2 all-gather.19
  473.6 41.9 all-gather.13
  518.7 295.9 all-gather.21
  820.6 41.9 all-gather.15
  1050.4 106.8 all-gather.23
